TPU v7x, 128 devices: a whole 4x4x4 slice. The times are simulated.
128 devices in a mesh: row: 8 (over z, core), col: 16 (over x, y).
Axes of the slice: x: 4, y: 4, z: 4, core: 2. Of those that a mesh axis runs over, the one named last changes fastest.
Arguments:
- normed: bfloat16 [8192, 7168], P(None, 'col'), may hold values from -44 to 44
- projection_weight: bfloat16 [7168, 3, 7168], P('col', None, 'row')
- adapter_down_weight: bfloat16 [7168, 16, 32], P(None, 'col'), may hold values from -0.0625 to 0.0625
- adapter_up_weight: bfloat16 [16, 2, 16, 7168], P(None, None, None, 'row'), may hold values from -0.47851562 to 0.47851562
- packed_prompt_length: int32 [64], replicated, may hold values from 64 to 512, as said below
- prompt_adapter_ids: int32 [64], replicated, may hold values from 0 to 63, as said below
- slot_adapter_ids: int32 [16], replicated, may hold values from 0 to 63, as said below
- prompt_page_slots: int32 [64, 4], replicated, may hold values from -1 to 159, as said below
Outputs:
- attended: bfloat16 [8192, 7168], P('col', 'row')
- kv_cache: bfloat16 [160, 128, 2, 7168], P('col', None, None, 'row')
Inputs may be any that keep to these rules, and one draw needn't show every extreme that they name: `packed_prompt_length`: the 64 lengths sum to 8192; one of them is exactly 512 and one exactly 64. `slot_adapter_ids`: distinct adapter ids. `prompt_adapter_ids`: every entry is one of slot_adapter_ids, and every loaded adapter is named by at least one prompt. `prompt_page_slots`: entry [i, j] is -1 where 128 * j >= packed_prompt_length[i]; otherwise it lies among slots 10 * c to 10 * c + 9, where c is the block of 512 packed tokens that holds the page's last token. No slot is named twice.
All inputs are finite; a program needn't handle non-finite values.
Results may differ from a plain program's by a relative error of at most 0.0072.
Values may be sent and summed in bfloat16 or wider, within the bound.
A program may use at most 256 MiB of HBM per device.

v0:
```python
import jax
import jax.numpy as jnp
from jax import lax
from jax.sharding import PartitionSpec as P

HEAD_DIM = 128
PAGE = 128
NEAR = 1
SLOTS_DEV = 10
adapter_scale = 2.0
masked_score = -1e30


def shifted(block, axis, distance):
    devices = range(lax.axis_size(axis))
    route = [(i - distance, i) for i in devices if i - distance in devices]
    return lax.ppermute(block, axis, route)


def start_table(packed_prompt_length):
    prompt_ends = jnp.cumsum(packed_prompt_length)
    return prompt_ends - packed_prompt_length


def slot_table(prompt_adapter_ids, slot_adapter_ids):
    active_slots = slot_adapter_ids.shape[0]
    matched = slot_adapter_ids[None, :] == prompt_adapter_ids[:, None]
    return jnp.sum(
        jnp.where(matched, jnp.arange(active_slots, dtype=jnp.int32)[None, :], 0), axis=1
    )


def token_prompts(positions, prompt_starts):
    inside = (positions[:, None] >= prompt_starts[None, :]).astype(jnp.int32)
    return jnp.sum(inside, axis=1) - 1


def token_slots(prompts, slot_of):
    prompt_count = slot_of.shape[0]
    onehot = prompts[:, None] == jnp.arange(prompt_count, dtype=jnp.int32)[None, :]
    return jnp.sum(jnp.where(onehot, slot_of[None, :], 0), axis=1)


def down_term(row_block, slots_here, down_cols, active_slots):
    combined_output = jnp.dot(row_block, down_cols, preferred_element_type=jnp.float32)
    combined_output = combined_output.reshape(row_block.shape[0], active_slots, -1)
    pick_slot = slots_here[:, None] == jnp.arange(active_slots, dtype=jnp.int32)[None, :]
    return jnp.sum(jnp.where(pick_slot[:, :, None], combined_output, 0.0), axis=1)


def local(
    normed,
    projection_weight,
    adapter_down_weight,
    adapter_up_weight,
    packed_prompt_length,
    prompt_adapter_ids,
    slot_adapter_ids,
    prompt_page_slots,
):
    col_count = lax.axis_size("col")
    row_count = lax.axis_size("row")
    col_index = lax.axis_index("col")
    my_row = lax.axis_index("row")
    tok_all, width_loc = normed.shape
    tok_blk = tok_all // col_count
    head_column_span = projection_weight.shape[2]
    heads_loc = head_column_span // HEAD_DIM
    active_slots = slot_adapter_ids.shape[0]
    adapter_rank_width = adapter_up_weight.shape[2]
    prompt_starts = start_table(packed_prompt_length)
    slot_of = slot_table(prompt_adapter_ids, slot_adapter_ids)
    block_start = col_index * tok_blk
    mine = block_start + jnp.arange(tok_blk, dtype=jnp.int32)
    mine_prompts = token_prompts(mine, prompt_starts)
    mine_slots = token_slots(mine_prompts, slot_of)
    down_weight_slices = lax.all_to_all(
        adapter_down_weight, "col", split_axis=0, concat_axis=1, tiled=True
    )
    down_cols = down_weight_slices.reshape(width_loc, -1)
    own_rows = lax.all_to_all(normed, "col", split_axis=0, concat_axis=1, tiled=True)
    weight_piece = lax.all_gather(projection_weight, "col", axis=0, tiled=True)
    flat_piece = weight_piece.reshape(weight_piece.shape[0], -1)
    projection_total = jnp.dot(own_rows, flat_piece, preferred_element_type=jnp.float32)
    rows_per = tok_all // row_count
    row_first = my_row * rows_per
    row_positions = row_first + jnp.arange(rows_per, dtype=jnp.int32)
    row_slots = token_slots(token_prompts(row_positions, prompt_starts), slot_of)
    row_part = lax.dynamic_slice_in_dim(normed, row_first, rows_per, 0)
    summed = lax.psum(down_term(row_part, row_slots, down_cols, active_slots), "col")
    down_every = lax.all_gather(summed.astype(jnp.bfloat16), "row", axis=0, tiled=True)
    local_down_output = lax.dynamic_slice_in_dim(down_every, block_start, tok_blk, 0)
    pick_half = (mine_slots[:, None] == jnp.arange(active_slots, dtype=jnp.int32)[None, :]).astype(
        jnp.bfloat16
    )

    def reduced_rank_rows(low_part, slot_membership):
        token_spread = (pick_half[:, :, None] * low_part[:, None, :]).reshape(
            tok_blk, active_slots * adapter_rank_width
        )
        up_weight_table = adapter_up_weight[:, slot_membership].reshape(
            active_slots * adapter_rank_width, head_column_span
        )
        return jnp.dot(token_spread, up_weight_table, preferred_element_type=jnp.float32)

    query_token_rows = (
        projection_total[:, :head_column_span]
        + adapter_scale * reduced_rank_rows(local_down_output[:, :adapter_rank_width], 0)
    ).astype(jnp.bfloat16)
    key_rows = projection_total[:, head_column_span : 2 * head_column_span].astype(jnp.bfloat16)
    value_token_rows = (
        projection_total[:, 2 * head_column_span :]
        + adapter_scale * reduced_rank_rows(local_down_output[:, adapter_rank_width:], 1)
    ).astype(jnp.bfloat16)
    own_kv = jnp.stack([key_rows, value_token_rows], axis=1)
    earlier = [shifted(own_kv, "col", 1)]
    window = jnp.concatenate(earlier[::-1] + [own_kv], axis=0)
    window_len = window.shape[0]
    window_pos = block_start - NEAR * tok_blk + jnp.arange(window_len, dtype=jnp.int32)
    window_prompts = token_prompts(window_pos, prompt_starts)
    allowed = (mine_prompts[:, None] == window_prompts[None, :]) & (
        window_pos[None, :] <= mine[:, None]
    )
    query_heads = query_token_rows.reshape(tok_blk, heads_loc, HEAD_DIM)
    key_heads = window[:, 0].reshape(window_len, heads_loc, HEAD_DIM)
    value_heads = window[:, 1].reshape(window_len, heads_loc, HEAD_DIM)
    score_scale = HEAD_DIM ** (-0.5)
    scores = (
        jnp.einsum("qhd,khd->hqk", query_heads, key_heads, preferred_element_type=jnp.float32)
        * score_scale
    )
    limited = jnp.where(allowed[None], scores, masked_score)
    peak_score = jnp.max(limited, axis=2, keepdims=True)
    weight = jnp.where(allowed[None], jnp.exp(scores - peak_score), 0.0)
    denominator = jnp.sum(weight, axis=2)
    mixed_heads = jnp.einsum(
        "hqk,khd->qhd", weight.astype(jnp.bfloat16), value_heads, preferred_element_type=jnp.float32
    )
    attended = (
        (mixed_heads / jnp.transpose(denominator)[:, :, None])
        .reshape(tok_blk, head_column_span)
        .astype(jnp.bfloat16)
    )
    prev_kv = earlier[0]
    page_window = jnp.concatenate(
        [prev_kv, own_kv, jnp.zeros((PAGE, 2, head_column_span), jnp.bfloat16)], axis=0
    )
    max_pages = prompt_page_slots.shape[1]
    lens_rep = jnp.repeat(packed_prompt_length, max_pages)
    starts_rep = jnp.repeat(prompt_starts, max_pages)
    page_index = jnp.tile(jnp.arange(max_pages, dtype=jnp.int32), packed_prompt_length.shape[0])
    page_rows = jnp.clip(lens_rep - PAGE * page_index, 0, PAGE)
    page_first = starts_rep + PAGE * page_index
    my_slots = col_index * SLOTS_DEV + jnp.arange(SLOTS_DEV, dtype=jnp.int32)
    slot_hit = prompt_page_slots.reshape(-1)[None, :] == my_slots[:, None]
    rows_used = jnp.sum(jnp.where(slot_hit, page_rows[None, :], 0), axis=1)
    first_used = jnp.sum(jnp.where(slot_hit, page_first[None, :], 0), axis=1)
    offset = jnp.clip(first_used - (col_index - 1) * tok_blk, 0, 2 * tok_blk)
    page_lines = jnp.arange(PAGE, dtype=jnp.int32)
    pick_rows = (offset[:, None] + page_lines[None, :]).reshape(-1)
    taken_rows = jnp.take(page_window, pick_rows, axis=0).reshape(
        SLOTS_DEV, PAGE, 2, head_column_span
    )
    live_rows = (page_lines[None, :] < rows_used[:, None])[:, :, None, None]
    kv_pages = jnp.where(live_rows, taken_rows, jnp.zeros_like(taken_rows))
    return (attended, kv_pages)


def solution(mesh):
    placed = (
        P(None, "col"),
        P("col", None, "row"),
        P(None, "col", None),
        P(None, None, None, "row"),
        P(),
        P(),
        P(),
        P(),
    )
    return jax.shard_map(
        local,
        mesh=mesh,
        in_specs=placed,
        out_specs=(P("col", "row"), P("col", None, None, "row")),
        check_vma=False,
    )
```

profile of v0, /device:TPU:6, one launch (start us, length us, event | category | flops | bytes accessed | tf_op | source)
XLA Modules:
  0.0 544.9 jit_solution(5829252045479823222)
XLA Ops:
  7.2 0.0 all-gather.2.cloned.1.call-start
  7.2 0.7 all-gather.2.cloned.1.call-update
  7.9 0.5 broadcast.227
  8.4 1.9 reduce.3
  10.3 0.9 copy.105
  11.3 2.4 reshape.319
  13.7 7.4 %all-to-all-start.1 = ((bf16[16,2,7168]{2,1,0:T(2,128)(2,1)}), bf16[16,2,7168]{2,1,0:T(2,128)(2,1)S(1)}, u32[]{:S(2)}, u32[]{:S(2)}) async-start(bf16[16,2,7168]{2,1,0:T(2,128)(2,1)} %reshape.319), calls=%async_computation.1 | async-start | bytes 917504 | tf_op jit(solution)/shard_map/all_to_all | solution.py:77
  21.1 8.1 %copy.104 = bf16[56,16,8,512]{3,2,0,1:T(8,128)(2,1)} copy(bf16[56,16,8,512]{3,2,1,0:T(8,128)(2,1)} %bitcast.61) | data formatting | bytes 14680064 | tf_op jit(solution)/shard_map/all_to_all | solution.py:81
  29.2 1.7 all-to-all-done.1
  31.0 5.9 %all-to-all-start = ((bf16[16,512,448]{1,2,0:T(8,128)(2,1)}), bf16[16,512,448]{1,2,0:T(8,128)(2,1)}, u32[]{:S(2)}, u32[]{:S(2)}) async-start(bf16[16,512,448]{1,2,0:T(8,128)(2,1)} %bitcast.59), calls=%async_computation | async-start | bytes 14680064 | tf_op jit(solution)/shard_map/all_to_all | solution.py:81
  36.9 0.0 copy-done.5
  36.9 0.1 copy.82
  37.0 0.1 reduce-window.9
  37.1 0.1 reduce
  37.3 0.0 copy-done.7
  37.3 0.0 copy-done.8
  37.3 0.1 select_reduce_fusion.4
  37.4 0.1 convert_reduce_fusion.2
  37.5 0.1 select_reduce_fusion.3
  37.6 0.1 convert_reduce_fusion
  37.7 0.1 select_reduce_fusion.2
  37.9 0.1 fusion.21
  38.0 0.1 subtract_clamp_fusion
  38.1 0.1 fusion.36
  38.1 4.2 reshape.320
  42.4 7.0 %copy.84 = bf16[7168,1,32]{0,2,1:T(8,128)(2,1)S(1)} copy(bf16[7168,1,32]{2,1,0:T(2,128)(2,1)} %reshape.320) | data formatting | bytes 917504 | tf_op jit(solution)/shard_map/all_to_all | solution.py:77
  49.4 0.6 all_to_all.30
  50.0 1.9 select_reduce_fusion.1
  52.0 199.3 %all-reduce.1 = bf16[1024,32]{0,1:T(8,128)(2,1)S(1)} all-reduce(f32[1024,32]{0,1:T(8,128)S(1)} %select_reduce_fusion.1), channel_id=1, replica_groups=mesh['row'=8,'col'=16] {'col'}, use_global_device_ids=true, to_apply=%region_7.8 | all-reduce | flops 32768 | bytes 196608 | tf_op jit(solution)/shard_map/psum | solution.py:90
  251.3 13.7 %all_gather.7 = bf16[8192,32]{0,1:T(8,128)(2,1)S(1)} all-gather(bf16[1024,32]{0,1:T(8,128)(2,1)S(1)} %all-reduce.1), channel_id=1, replica_groups=mesh['row'=8,'col'=16] {'row'}, dimensions={0}, use_global_device_ids=true | all-gather | bytes 589824 | tf_op jit(solution)/shard_map/all_gather | solution.py:91
  265.0 66.0 %all-gather.2.cloned.1.call-done = bf16[7168,3,896]{2,0,1:T(8,128)(2,1)} async-done(((bf16[448,3,896]{2,0,1:T(8,128)(2,1)}), bf16[7168,3,896]{2,0,1:T(8,128)(2,1)}) %all-gather.2.cloned.1.call-update) | async-done | bytes 38535184 | tf_op jit(solution)/shard_map/all_gather | solution.py:82
  331.0 51.4 %copy.81 = bf16[7168,3,896]{0,2,1:T(8,128)(2,1)} copy(bf16[7168,3,896]{2,0,1:T(8,128)(2,1)} %all-gather.2.cloned.1.call-done) | data formatting | bytes 77070336 | tf_op jit(solution)/shard_map/all_gather | solution.py:82
  382.4 0.0 all-to-all-done
  382.4 28.4 %fusion.38 = f32[512,2688]{1,0:T(8,128)} fusion(bf16[512,7168]{0,1:T(8,128)(2,1)} %bitcast.1, bf16[7168,2688]{0,1:T(8,128)(2,1)} %bitcast.58), kind=kOutput, calls=%fused_computation.78 | convolution fusion | flops 19730006016 | bytes 51380224 | tf_op jit(solution)/shard_map/dot_general | solution.py:84
  410.8 1.6 fusion.16
  412.4 2.0 fusion.15
  414.3 1.4 pad_maximum_fusion
  415.8 1.9 collective-permute-start
  417.7 0.1 copy.91
  417.8 0.1 eq.123
  417.9 0.1 add.145
  418.0 0.1 min.20
  418.1 0.2 fusion.24
  418.3 0.1 fusion.25
  418.5 0.1 fusion.28
  418.5 0.1 iota_compare_fusion.4
  418.6 1.3 compare_and_fusion
  419.9 2.0 fusion.10
  421.9 1.5 copy.87
  423.4 41.3 %collective-permute-done = bf16[512,2,896]{2,0,1:T(8,128)(2,1)} collective-permute-done((bf16[512,2,896]{2,0,1:T(8,128)(2,1)}, bf16[512,2,896]{2,0,1:T(8,128)(2,1)}, u32[]{:S(2)}, u32[]{:S(2)}) %collective-permute-start) | collective-permute-done | bytes 1835040 | tf_op jit(solution)/shard_map/ppermute | solution.py:17
  464.7 1.8 maximum_maximum_fusion.1
  466.5 2.1 fusion.35
  468.6 3.8 copy.88
  472.5 3.1 maximum_maximum_fusion
  475.6 0.0 copy-start.3
  475.7 15.3 %copy.92 = bf16[1152,2,896]{2,1,0:T(2,128)(2,1)} copy(bf16[1152,2,896]{2,0,1:T(8,128)(2,1)S(1)} %maximum_maximum_fusion) | data formatting | bytes 8257536 | tf_op jit(solution)/shard_map/concatenate | solution.py:145
  490.9 0.0 copy-done
  490.9 2.4 copy.86
  493.3 0.0 copy-done.4
  493.3 12.7 %fusion.37 = (f32[7,512]{1,0:T(8,128)S(1)}, bf16[7,512,1024]{2,1,0:T(8,128)(2,1)}) fusion(pred[512,1024]{1,0:T(8,128)(4,1)S(1)} %copy-done.4, bf16[512,7,128]{0,2,1:T(8,128)(2,1)S(1)} %bitcast.68, bf16[1024,7,128]{0,2,1:T(8,128)(2,1)} %bitcast.62), kind=kOutput, calls=%fused_computation.77 | convolution fusion | flops 1904739328 | bytes 10631168 | tf_op jit(solution)/shard_map/sub | solution.py:134
  506.0 5.7 %fusion.12 = bf16[512,7,128]{0,2,1:T(8,128)(2,1)S(1)} fusion(bf16[1024,7,128]{0,2,1:T(8,128)(2,1)S(1)} %bitcast.63, bf16[7,512,1024]{2,1,0:T(8,128)(2,1)} %get-tuple-element.29, f32[512,7]{0,1:T(8,128)S(1)} %bitcast.72), kind=kOutput, calls=%fused_computation.25 | convolution fusion | flops 940441600 | bytes 10106880 | tf_op jit(solution)/shard_map/hqk,khd->qhd/dot_general | solution.py:136
  511.7 1.3 copy.93
  513.0 16.6 %gather_fusion = bf16[1280,2,896]{2,1,0:T(2,128)(2,1)} fusion(bf16[1152,2,896]{2,1,0:T(2,128)(2,1)} %copy.92, s32[2048]{0:T(1024)S(1)} %pad_clamp_fusion), kind=kCustom, calls=%fused_computation | custom fusion | bytes 9180160 | tf_op jit(solution)/shard_map/jit(_take)/gather | solution.py:161
  529.6 8.5 %broadcast_select_fusion.1 = bf16[10,128,2,896]{3,2,1,0:T(2,128)(2,1)} fusion(pred[10,128]{1,0:T(8,128)(4,1)S(1)} %iota_compare_fusion.4, bf16[10,128,2,896]{3,2,1,0:T(2,128)(2,1)} %bitcast.60, pred[10,128]{1,0:T(8,128)(4,1)S(1)} %fusion.28), kind=kLoop, calls=%fused_computation.7 | loop fusion | flops 4587520 | bytes 9177600 | tf_op jit(solution)/shard_map/jit(_where)/select_n | solution.py:165
  (28 shorter events, 0.2 us)
Async XLA Ops:
  7.2 323.8 %all-gather.2.cloned.1.call-start = ((), (), s32[]{:S(2)}) async-start(), calls=%async_computation.2 | async-start | bytes 40943616 | tf_op jit(solution)/shard_map/all_gather | solution.py:82
  13.7 17.3 %all-to-all-start.1 = ((bf16[16,2,7168]{2,1,0:T(2,128)(2,1)}), bf16[16,2,7168]{2,1,0:T(2,128)(2,1)S(1)}, u32[]{:S(2)}, u32[]{:S(2)}) async-start(bf16[16,2,7168]{2,1,0:T(2,128)(2,1)} %reshape.319), calls=%async_computation.1 | async-start | bytes 917504 | tf_op jit(solution)/shard_map/all_to_all | solution.py:77
  31.0 5.9 %copy-start.5 = (s32[64]{0:T(128)S(1)}, s32[64]{0:T(128)}, u32[]{:S(2)}) copy-start(s32[64]{0:T(128)} %param.12) | copy-start | bytes 772
  31.0 6.3 %copy-start.7 = (s32[64]{0:T(128)S(1)}, s32[64]{0:T(128)}, u32[]{:S(2)}) copy-start(s32[64]{0:T(128)} %param.13) | copy-start | bytes 772
  31.0 6.3 %copy-start.8 = (s32[16]{0:T(128)S(1)}, s32[16]{0:T(128)}, u32[]{:S(2)}) copy-start(s32[16]{0:T(128)} %param.14) | copy-start | bytes 196
  31.0 7.1 %copy-start.2 = (bf16[16,2,16,896]{3,2,1,0:T(8,128)(2,1)S(1)}, bf16[16,2,16,896]{3,2,1,0:T(8,128)(2,1)}, u32[]{:S(2)}) copy-start(bf16[16,2,16,896]{3,2,1,0:T(8,128)(2,1)} %param.11) | copy-start | bytes 2752516
  31.0 351.4 %all-to-all-start = ((bf16[16,512,448]{1,2,0:T(8,128)(2,1)}), bf16[16,512,448]{1,2,0:T(8,128)(2,1)}, u32[]{:S(2)}, u32[]{:S(2)}) async-start(bf16[16,512,448]{1,2,0:T(8,128)(2,1)} %bitcast.59), calls=%async_computation | async-start | bytes 14680064 | tf_op jit(solution)/shard_map/all_to_all | solution.py:81
  410.8 6.9 %copy-start.6 = (s32[64,4]{0,1:T(4,128)S(1)}, s32[64,4]{0,1:T(4,128)}, u32[]{:S(2)}) copy-start(s32[64,4]{0,1:T(4,128)} %param.15) | copy-start | bytes 3076
  415.8 49.0 %collective-permute-start = (bf16[512,2,896]{2,0,1:T(8,128)(2,1)}, bf16[512,2,896]{2,0,1:T(8,128)(2,1)}, u32[]{:S(2)}, u32[]{:S(2)}) collective-permute-start(bf16[512,2,896]{2,0,1:T(8,128)(2,1)} %pad_maximum_fusion), channel_id=1, source_target_pairs={{0,1},{1,2},{2,3},{3,4},{4,5},{5,6},{6,7},{7,8},{8,9},{9,10},{10,1... | collective-permute-start | bytes 5505032 | tf_op jit(solution)/shard_map/ppermute | solution.py:17
  475.6 15.3 %copy-start = (bf16[1024,1,896]{2,0,1:T(8,128)(2,1)S(1)}, bf16[1024,1,896]{2,0,1:T(8,128)(2,1)}, u32[]{:S(2)}) copy-start(bf16[1024,1,896]{2,0,1:T(8,128)(2,1)} %get-tuple-element.21) | copy-start | bytes 5505028
  475.6 17.7 %copy-start.3 = (bf16[512,896]{0,1:T(8,128)(2,1)S(1)}, bf16[512,896]{0,1:T(8,128)(2,1)}, u32[]{:S(2)}) copy-start(bf16[512,896]{0,1:T(8,128)(2,1)} %copy.87) | copy-start | bytes 2752516
  475.6 17.7 %copy-start.4 = (pred[512,1024]{1,0:T(8,128)(4,1)S(1)}, pred[512,1024]{1,0:T(8,128)(4,1)}, u32[]{:S(2)}) copy-start(pred[512,1024]{1,0:T(8,128)(4,1)} %compare_and_fusion) | copy-start | bytes 1572868
  493.3 12.7 %copy-start.1 = (bf16[1024,1,896]{0,2,1:T(8,128)(2,1)S(1)}, bf16[1024,1,896]{0,2,1:T(8,128)(2,1)}, u32[]{:S(2)}) copy-start(bf16[1024,1,896]{0,2,1:T(8,128)(2,1)} %copy.86) | copy-start | bytes 5505028
Sparse Core Ops, SparseCore 0:
  10.1 320.8 all-gather.1
where the time goes:
time: 547 us; the launch traced here: 545 us
  blocking collectives  213 us (39%)
  local copies, waits for them, and re-layouts  120 us (22%)
  waiting for transfers between devices  110 us (20%)
  matrix products  52.6 us (10%)
  other arithmetic  19.5 us (4%)
  starting transfers between devices  15.3 us (3%)
  between operations  14.3 us (3%)
    psum x1, blocking collectives, local(): lax.psum(down_term(row_part, row_slots, down_cols, active_slots), 'col')  199 us
    all_gather x1, waiting for transfers between devices, local(): weight_piece = lax.all_gather(projection_weight, 'col', axis=0, tiled=True)  66 us
    all_gather x1, local copies, waits for them, and re-layouts, local(): weight_piece = lax.all_gather(projection_weight, 'col', axis=0, tiled=True)  51.4 us
    ppermute x1, waiting for transfers between devices, shifted(): return lax.ppermute(block, axis, route)  41.3 us
    dot_general x1, matrix products, local(): jnp.dot(own_rows, flat_piece, preferred_element_type=jnp.float32)  28.4 us
    gather x1, local copies, waits for them, and re-layouts, local(): jnp.take(page_window, pick_rows, axis=0)  16.6 us
    concatenate x2, local copies, waits for them, and re-layouts, local(): jnp.concatenate([prev_kv, own_kv, jnp.zeros((PAGE, 2, head_column_span),...  15.3 us
    all_gather x1, blocking collectives, local(): lax.all_gather(summed.astype(jnp.bfloat16), 'row', axis=0, tiled=True)  13.7 us
  transfers between devices with their start and end apart: 4, of which 3 were waited for; matrix products, arithmetic and copies ran while one was open for 16% of the time, Pallas kernels for 0%

commit v1 on v0

--- a/solution.py
+++ b/solution.py
@@ -87,7 +87,9 @@
     row_positions = row_first + jnp.arange(rows_per, dtype=jnp.int32)
     row_slots = token_slots(token_prompts(row_positions, prompt_starts), slot_of)
     row_part = lax.dynamic_slice_in_dim(normed, row_first, rows_per, 0)
-    summed = lax.psum(down_term(row_part, row_slots, down_cols, active_slots), "col")
+    summed = jnp.sum(
+        lax.all_gather(down_term(row_part, row_slots, down_cols, active_slots), "col"), axis=0
+    )
     down_every = lax.all_gather(summed.astype(jnp.bfloat16), "row", axis=0, tiled=True)
     local_down_output = lax.dynamic_slice_in_dim(down_every, block_start, tok_blk, 0)
     pick_half = (mine_slots[:, None] == jnp.arange(active_slots, dtype=jnp.int32)[None, :]).astype(

time: 547 us -> 617 us (1.13)
  waiting for transfers between devices: 110 us -> 374 us
  blocking collectives: 213 us -> 15.2 us
    psum x1 -> x0, blocking collectives: 199 us -> none  [local(): lax.psum(down_term(row_part, row_slots, down_cols, active_slots), 'col')]
    all_gather x1, waiting for transfers between devices: 66 us -> 222 us  [local(): weight_piece = lax.all_gather(projection_weight, 'col', axis=0, tiled=True)]
    all_gather x0 -> x1, waiting for transfers between devices: none -> 105 us  [local(): lax.all_gather(down_term(row_part, row_slots, down_cols, active_slots), '...]
    all_to_all x1, waiting for transfers between devices: 1.74 us -> 7.99 us  [local(): lax.all_to_all(adapter_down_weight, 'col', split_axis=0, concat_axis=1, t...]
  transfers between devices with their start and end apart: 4 -> 5, of which waited for: 3 -> 4; matrix products, arithmetic and copies ran while one was open for 16% -> 11% of each run, Pallas kernels for 0% -> 0%
where the time goes in v1:
time: 617 us; the launch traced here: 615 us
  waiting for transfers between devices  374 us (61%)
  local copies, waits for them, and re-layouts  122 us (20%)
  matrix products  53.3 us (9%)
  other arithmetic  19.8 us (3%)
  starting transfers between devices  16.4 us (3%)
  blocking collectives  15.2 us (2%)
  between operations  14.4 us (2%)
    all_gather x1, waiting for transfers between devices, local(): weight_piece = lax.all_gather(projection_weight, 'col', axis=0, tiled=True)  222 us
    all_gather x1, waiting for transfers between devices, local(): lax.all_gather(down_term(row_part, row_slots, down_cols, active_slots), '...  105 us
    all_gather x1, local copies, waits for them, and re-layouts, local(): weight_piece = lax.all_gather(projection_weight, 'col', axis=0, tiled=True)  51.5 us
    ppermute x1, waiting for transfers between devices, shifted(): return lax.ppermute(block, axis, route)  38.2 us
    dot_general x1, matrix products, local(): jnp.dot(own_rows, flat_piece, preferred_element_type=jnp.float32)  28.4 us
    gather x1, local copies, waits for them, and re-layouts, local(): jnp.take(page_window, pick_rows, axis=0)  16.6 us
    concatenate x2, local copies, waits for them, and re-layouts, local(): jnp.concatenate([prev_kv, own_kv, jnp.zeros((PAGE, 2, head_column_span),...  15.3 us
    all_gather x1, blocking collectives, local(): lax.all_gather(summed.astype(jnp.bfloat16), 'row', axis=0, tiled=True)  15.2 us
  transfers between devices with their start and end apart: 5, of which 4 were waited for; matrix products, arithmetic and copies ran while one was open for 11% of the time, Pallas kernels for 0%

profile of v1, /device:TPU:6, one launch (start us, length us, event | category | flops | bytes accessed | tf_op | source)
XLA Modules:
  0.0 614.7 jit_solution(6641930894091566892)
XLA Ops:
  7.2 0.5 broadcast.227
  7.7 1.9 reduce.3
  9.6 0.9 copy.106
  10.6 2.4 reshape.320
  13.0 7.4 %all-to-all-start.1 = ((bf16[16,2,7168]{2,1,0:T(2,128)(2,1)}), bf16[16,2,7168]{2,1,0:T(2,128)(2,1)S(1)}, u32[]{:S(2)}, u32[]{:S(2)}) async-start(bf16[16,2,7168]{2,1,0:T(2,128)(2,1)} %reshape.320), calls=%async_computation.1 | async-start | bytes 917504 | tf_op jit(solution)/shard_map/all_to_all | solution.py:77
  20.4 0.0 all-gather.6.cloned.1.call-start
  20.5 0.1 copy.82
  20.6 0.1 reduce-window.9
  20.7 0.1 reduce
  20.8 0.1 convert_reduce_fusion
  21.0 0.1 select_reduce_fusion.4
  21.1 0.1 select_reduce_fusion.2
  21.2 8.0 %all-to-all-done.1 = bf16[16,2,7168]{2,1,0:T(2,128)(2,1)S(1)} async-done(((bf16[16,2,7168]{2,1,0:T(2,128)(2,1)}), bf16[16,2,7168]{2,1,0:T(2,128)(2,1)S(1)}, u32[]{:S(2)}, u32[]{:S(2)}) %all-to-all-start.1) | async-done | bytes 458784 | tf_op jit(solution)/shard_map/all_to_all | solution.py:77
  29.2 4.2 reshape.321
  33.5 7.0 %copy.84 = bf16[7168,1,32]{0,2,1:T(8,128)(2,1)S(1)} copy(bf16[7168,1,32]{2,1,0:T(2,128)(2,1)} %reshape.321) | data formatting | bytes 917504 | tf_op jit(solution)/shard_map/all_to_all | solution.py:77
  40.5 0.6 all_to_all.30
  41.1 2.6 select_reduce_fusion.1
  43.7 0.0 all-gather.6.cloned.1.call-update
  43.7 0.0 all-gather.4.cloned.1.call-start
  43.8 0.7 all-gather.4.cloned.1.call-update
  44.5 6.8 %copy.105 = bf16[56,16,8,512]{3,2,0,1:T(8,128)(2,1)} copy(bf16[56,16,8,512]{3,2,1,0:T(8,128)(2,1)} %bitcast.66) | data formatting | bytes 14680064 | tf_op jit(solution)/shard_map/all_to_all | solution.py:81
  51.3 6.7 %all-to-all-start = ((bf16[16,512,448]{1,2,0:T(8,128)(2,1)}), bf16[16,512,448]{1,2,0:T(8,128)(2,1)}, u32[]{:S(2)}, u32[]{:S(2)}) async-start(bf16[16,512,448]{1,2,0:T(8,128)(2,1)} %bitcast.64), calls=%async_computation | async-start | bytes 14680064 | tf_op jit(solution)/shard_map/all_to_all | solution.py:81
  58.0 0.1 convert_reduce_fusion.2
  58.1 0.1 select_reduce_fusion.3
  58.2 0.1 fusion.21
  58.3 0.1 subtract_clamp_fusion
  58.4 0.1 fusion.36
  58.5 104.7 %all-gather.6.cloned.1.call-done = f32[16384,32]{0,1:T(8,128)} async-done(((f32[1024,32]{0,1:T(8,128)}), f32[16384,32]{0,1:T(8,128)}) %all-gather.6.cloned.1.call-update) | async-done | bytes 2097168 | tf_op jit(solution)/shard_map/all_gather | solution.py:91
  163.2 2.8 copy.97
  166.0 0.3 bitcast_reduce_fusion
  166.3 15.2 %all_gather.15 = bf16[8192,32]{0,1:T(8,128)(2,1)S(1)} all-gather(bf16[1024,32]{0,1:T(8,128)(2,1)S(1)} %bitcast_reduce_fusion), channel_id=1, replica_groups=mesh['row'=8,'col'=16] {'row'}, dimensions={0}, use_global_device_ids=true | all-gather | bytes 589824 | tf_op jit(solution)/shard_map/all_gather | solution.py:93
  181.6 222.0 %all-gather.4.cloned.1.call-done = bf16[7168,3,896]{2,0,1:T(8,128)(2,1)} async-done(((bf16[448,3,896]{2,0,1:T(8,128)(2,1)}), bf16[7168,3,896]{2,0,1:T(8,128)(2,1)}) %all-gather.4.cloned.1.call-update) | async-done | bytes 38535184 | tf_op jit(solution)/shard_map/all_gather | solution.py:82
  403.6 51.5 %copy.81 = bf16[7168,3,896]{0,2,1:T(8,128)(2,1)} copy(bf16[7168,3,896]{2,0,1:T(8,128)(2,1)} %all-gather.4.cloned.1.call-done) | data formatting | bytes 77070336 | tf_op jit(solution)/shard_map/all_gather | solution.py:82
  455.1 0.0 all-to-all-done
  455.1 28.4 %fusion.38 = f32[512,2688]{1,0:T(8,128)} fusion(bf16[512,7168]{0,1:T(8,128)(2,1)} %bitcast.1, bf16[7168,2688]{0,1:T(8,128)(2,1)} %bitcast.63), kind=kOutput, calls=%fused_computation.79 | convolution fusion | flops 19730006016 | bytes 51380224 | tf_op jit(solution)/shard_map/dot_general | solution.py:84
  483.5 1.6 fusion.16
  485.1 2.0 fusion.15
  487.0 1.4 pad_maximum_fusion
  488.4 2.2 collective-permute-start
  490.6 0.0 copy-done.6
  490.7 0.1 copy.91
  490.8 0.1 eq.123
  490.9 0.1 add.143
  491.0 0.1 min.20
  491.1 0.2 fusion.24
  491.3 0.1 fusion.25
  491.4 0.1 fusion.28
  491.5 0.1 iota_compare_fusion.4
  491.6 1.3 compare_and_fusion
  492.9 2.0 fusion.10
  494.8 1.5 copy.87
  496.3 38.2 %collective-permute-done = bf16[512,2,896]{2,0,1:T(8,128)(2,1)} collective-permute-done((bf16[512,2,896]{2,0,1:T(8,128)(2,1)}, bf16[512,2,896]{2,0,1:T(8,128)(2,1)}, u32[]{:S(2)}, u32[]{:S(2)}) %collective-permute-start) | collective-permute-done | bytes 1835040 | tf_op jit(solution)/shard_map/ppermute | solution.py:17
  534.5 1.8 maximum_maximum_fusion.1
  536.3 2.1 fusion.35
  538.5 3.8 copy.88
  542.3 3.1 maximum_maximum_fusion
  545.5 0.0 copy-start.3
  545.5 15.3 %copy.92 = bf16[1152,2,896]{2,1,0:T(2,128)(2,1)} copy(bf16[1152,2,896]{2,0,1:T(8,128)(2,1)S(1)} %maximum_maximum_fusion) | data formatting | bytes 8257536 | tf_op jit(solution)/shard_map/concatenate | solution.py:147
  560.8 2.4 copy.86
  563.2 12.7 %fusion.37 = (f32[7,512]{1,0:T(8,128)S(1)}, bf16[7,512,1024]{2,1,0:T(8,128)(2,1)}) fusion(pred[512,1024]{1,0:T(8,128)(4,1)S(1)} %copy-done.4, bf16[512,7,128]{0,2,1:T(8,128)(2,1)S(1)} %bitcast.74, bf16[1024,7,128]{0,2,1:T(8,128)(2,1)} %bitcast.68), kind=kOutput, calls=%fused_computation.78 | convolution fusion | flops 1904739328 | bytes 10631168 | tf_op jit(solution)/shard_map/sub | solution.py:136
  575.9 5.7 fusion.12
  581.5 1.3 copy.93
  582.8 16.6 %gather_fusion = bf16[1280,2,896]{2,1,0:T(2,128)(2,1)} fusion(bf16[1152,2,896]{2,1,0:T(2,128)(2,1)} %copy.92, s32[2048]{0:T(1024)S(1)} %pad_clamp_fusion), kind=kCustom, calls=%fused_computation | custom fusion | bytes 9180160 | tf_op jit(solution)/shard_map/jit(_take)/gather | solution.py:163
  599.4 8.5 %broadcast_select_fusion.1 = bf16[10,128,2,896]{3,2,1,0:T(2,128)(2,1)} fusion(pred[10,128]{1,0:T(8,128)(4,1)S(1)} %iota_compare_fusion.4, bf16[10,128,2,896]{3,2,1,0:T(2,128)(2,1)} %bitcast.65, pred[10,128]{1,0:T(8,128)(4,1)S(1)} %fusion.28), kind=kLoop, calls=%fused_computation.7 | loop fusion | flops 4587520 | bytes 9177600 | tf_op jit(solution)/shard_map/jit(_where)/select_n | solution.py:167
  (32 shorter events, 0.2 us)
Async XLA Ops:
  7.2 13.4 %copy-start.5 = (s32[64]{0:T(128)S(1)}, s32[64]{0:T(128)}, u32[]{:S(2)}) copy-start(s32[64]{0:T(128)} %param.12) | copy-start | bytes 772
  7.2 13.8 %copy-start.8 = (s32[16]{0:T(128)S(1)}, s32[16]{0:T(128)}, u32[]{:S(2)}) copy-start(s32[16]{0:T(128)} %param.14) | copy-start | bytes 196
  7.2 13.8 %copy-start.7 = (s32[64]{0:T(128)S(1)}, s32[64]{0:T(128)}, u32[]{:S(2)}) copy-start(s32[64]{0:T(128)} %param.13) | copy-start | bytes 772
  13.0 16.2 %all-to-all-start.1 = ((bf16[16,2,7168]{2,1,0:T(2,128)(2,1)}), bf16[16,2,7168]{2,1,0:T(2,128)(2,1)S(1)}, u32[]{:S(2)}, u32[]{:S(2)}) async-start(bf16[16,2,7168]{2,1,0:T(2,128)(2,1)} %reshape.320), calls=%async_computation.1 | async-start | bytes 917504 | tf_op jit(solution)/shard_map/all_to_all | solution.py:77
  20.4 142.7 %all-gather.6.cloned.1.call-start = ((), (), s32[]{:S(2)}) async-start(), calls=%async_computation.3 | async-start | bytes 2228224 | tf_op jit(solution)/shard_map/all_gather | solution.py:91
  43.7 359.9 %all-gather.4.cloned.1.call-start = ((), (), s32[]{:S(2)}) async-start(), calls=%async_computation.2 | async-start | bytes 40943616 | tf_op jit(solution)/shard_map/all_gather | solution.py:82
  51.3 7.1 %copy-start.2 = (bf16[16,2,16,896]{3,2,1,0:T(8,128)(2,1)S(1)}, bf16[16,2,16,896]{3,2,1,0:T(8,128)(2,1)}, u32[]{:S(2)}) copy-start(bf16[16,2,16,896]{3,2,1,0:T(8,128)(2,1)} %param.11) | copy-start | bytes 2752516
  51.3 403.8 %all-to-all-start = ((bf16[16,512,448]{1,2,0:T(8,128)(2,1)}), bf16[16,512,448]{1,2,0:T(8,128)(2,1)}, u32[]{:S(2)}, u32[]{:S(2)}) async-start(bf16[16,512,448]{1,2,0:T(8,128)(2,1)} %bitcast.64), calls=%async_computation | async-start | bytes 14680064 | tf_op jit(solution)/shard_map/all_to_all | solution.py:81
  483.5 7.2 %copy-start.6 = (s32[64,4]{0,1:T(4,128)S(1)}, s32[64,4]{0,1:T(4,128)}, u32[]{:S(2)}) copy-start(s32[64,4]{0,1:T(4,128)} %param.15) | copy-start | bytes 3076
  488.4 46.1 %collective-permute-start = (bf16[512,2,896]{2,0,1:T(8,128)(2,1)}, bf16[512,2,896]{2,0,1:T(8,128)(2,1)}, u32[]{:S(2)}, u32[]{:S(2)}) collective-permute-start(bf16[512,2,896]{2,0,1:T(8,128)(2,1)} %pad_maximum_fusion), channel_id=1, source_target_pairs={{0,1},{1,2},{2,3},{3,4},{4,5},{5,6},{6,7},{7,8},{8,9},{9,10},{10,1... | collective-permute-start | bytes 5505032 | tf_op jit(solution)/shard_map/ppermute | solution.py:17
  545.4 15.3 %copy-start = (bf16[1024,1,896]{2,0,1:T(8,128)(2,1)S(1)}, bf16[1024,1,896]{2,0,1:T(8,128)(2,1)}, u32[]{:S(2)}) copy-start(bf16[1024,1,896]{2,0,1:T(8,128)(2,1)} %get-tuple-element.21) | copy-start | bytes 5505028
  545.5 17.7 %copy-start.3 = (bf16[512,896]{0,1:T(8,128)(2,1)S(1)}, bf16[512,896]{0,1:T(8,128)(2,1)}, u32[]{:S(2)}) copy-start(bf16[512,896]{0,1:T(8,128)(2,1)} %copy.87) | copy-start | bytes 2752516
  545.5 17.7 %copy-start.4 = (pred[512,1024]{1,0:T(8,128)(4,1)S(1)}, pred[512,1024]{1,0:T(8,128)(4,1)}, u32[]{:S(2)}) copy-start(pred[512,1024]{1,0:T(8,128)(4,1)} %compare_and_fusion) | copy-start | bytes 1572868
  563.2 12.7 %copy-start.1 = (bf16[1024,1,896]{0,2,1:T(8,128)(2,1)S(1)}, bf16[1024,1,896]{0,2,1:T(8,128)(2,1)}, u32[]{:S(2)}) copy-start(bf16[1024,1,896]{0,2,1:T(8,128)(2,1)} %copy.86) | copy-start | bytes 5505028
Sparse Core Ops, SparseCore 0:
  43.8 119.2 all-gather.5
  165.3 238.2 all-gather.3
